TPU v7x, 32 devices: a whole 2x2x4 slice. The times are simulated.
32 devices in a mesh: dp: 8 (over z, y), tp: 4 (over x, core).
Axes of the slice: x: 2, y: 2, z: 4, core: 2. Of those that a mesh axis runs over, the one named last changes fastest.
Arguments:
- tokens: bfloat16 [128, 256, 512], P('dp'), may hold values from -6 to 6
- frame_counts: int32 [128], P('dp'), may hold values from 128 to 256, as said below
- rate_groups: int32 [128], P('dp'), may hold values from 0 to 1
- conv_weight: bfloat16 [7, 512], replicated, may hold values from -2 to 2
- conv_bias: bfloat16 [512], replicated, may hold values from -3 to 3
- norm_scale: bfloat16 [2, 512], replicated, may hold values from 0.5 to 1.5
- norm_shift: bfloat16 [2, 512], replicated, may hold values from -2 to 2
- weight_in: bfloat16 [512, 1536], P(None, 'tp'), may hold values from -0.25 to 0.25
- bias_in: bfloat16 [1536], P('tp'), may hold values from -2 to 2
- weight_out: bfloat16 [1536, 512], P('tp'), may hold values from -0.21875 to 0.21875
- bias_out: bfloat16 [512], replicated, may hold values from -2 to 2
- layer_scale: bfloat16 [512], replicated, may hold values from 0.5 to 1.5
- cotangent: bfloat16 [128, 256, 512], P('dp'), may hold values from -6 to 6
Outputs:
- block_out: bfloat16 [128, 256, 512], P('dp')
- grad_tokens: float32 [128, 256, 512], P('dp')
- grad_conv_weight: float32 [7, 512], replicated
- grad_conv_bias: float32 [512], replicated
- grad_norm_scale: float32 [2, 512], replicated
- grad_norm_shift: float32 [2, 512], replicated
- grad_weight_in: float32 [512, 1536], P(None, 'tp')
- grad_bias_in: float32 [1536], P('tp')
- grad_weight_out: float32 [1536, 512], P('tp')
- grad_bias_out: float32 [512], replicated
- grad_layer_scale: float32 [512], replicated
Inputs may be any that keep to these rules, and one draw needn't show every extreme that they name: `frame_counts`: an item of group 0 has at most 256 live frames, one of group 1 at most 240; both bounds are reached, and so is the least.
All inputs are finite; a program needn't handle non-finite values.
Results may differ from a plain program's by a relative error of at most 0.0061.
Values may be sent and summed in bfloat16 or wider, within the bound.
No kernel may reach another device: no remote copies, remote signals or barrier semaphores. Data moves between devices by JAX's collectives and lax.ppermute only.
A program may use at most 192 MiB of HBM per device.

v0:
```python
import jax
import jax.numpy as jnp
from jax import lax
from jax.sharding import PartitionSpec as P

EPS = 1e-06
HIGH = lax.Precision.HIGHEST


def gelu_parts(pre_act):
    normal_cdf = 0.5 * (1.0 + lax.erf(pre_act * 0.7071067811865476))
    density = jnp.exp(-0.5 * pre_act * pre_act) * 0.3989422804014327
    return (pre_act * normal_cdf, normal_cdf + pre_act * density)


def contract_rows(left, right, precision=None):
    return lax.dot_general(
        left,
        right,
        (((0,), (0,)), ((), ())),
        precision=precision,
        preferred_element_type=jnp.float32,
    )


def contract_last(left, right):
    return lax.dot_general(
        left, right, (((1,), (1,)), ((), ())), preferred_element_type=jnp.float32
    )


def per_device(
    tokens,
    frame_counts,
    rate_groups,
    conv_weight,
    conv_bias,
    norm_scale,
    norm_shift,
    weight_in,
    bias_in,
    weight_out,
    bias_out,
    layer_scale,
    cotangent,
):
    item_count, frames, model_width = tokens.shape
    row_count = item_count * frames
    tap_count = conv_weight.shape[0]
    half_width = tap_count // 2
    rate_count = norm_scale.shape[0]
    frame_mask = (jnp.arange(frames)[None, :] < frame_counts[:, None]).astype(jnp.float32)
    masked = tokens.astype(jnp.float32) * frame_mask[..., None]
    padded = jnp.pad(masked, ((0, 0), (half_width, half_width), (0, 0)))
    conv_taps = conv_weight.astype(jnp.float32)
    conv = conv_bias.astype(jnp.float32) + conv_taps[0] * padded[:, 0:frames]
    for tap_index in range(1, tap_count):
        conv = conv + conv_taps[tap_index] * padded[:, tap_index : tap_index + frames]
    row_mean = jnp.mean(conv, axis=-1, keepdims=True)
    centered = conv - row_mean
    variance = jnp.mean(centered * centered, axis=-1, keepdims=True)
    inv_std = lax.rsqrt(variance + EPS).reshape(row_count, 1)
    normed = centered.reshape(row_count, model_width) * inv_std
    hot_items = (rate_groups[:, None] == jnp.arange(rate_count)[None, :]).astype(jnp.float32)
    hot_rows = jnp.broadcast_to(hot_items[:, None, :], (item_count, frames, rate_count)).reshape(
        row_count, rate_count
    )
    scale_table = norm_scale.astype(jnp.float32)
    shift_table = norm_shift.astype(jnp.float32)
    scale_items = jnp.dot(hot_items, scale_table, precision=HIGH)
    shift_items = jnp.dot(hot_items, shift_table, precision=HIGH)
    adapted = (
        (
            normed.reshape(item_count, frames, model_width) * scale_items[:, None, :]
            + shift_items[:, None, :]
        )
        .astype(jnp.bfloat16)
        .reshape(row_count, model_width)
    )
    pre_act = jnp.dot(adapted, weight_in, preferred_element_type=jnp.float32) + bias_in.astype(
        jnp.float32
    )
    activation, gelu_slope = gelu_parts(pre_act)
    act_low = activation.astype(jnp.bfloat16)
    masked_rows = masked.reshape(row_count, model_width)
    mask_rows = frame_mask.reshape(row_count, 1)
    grad_rows = cotangent.astype(jnp.float32).reshape(row_count, model_width) * mask_rows
    gamma = layer_scale.astype(jnp.float32)
    bias_last = bias_out.astype(jnp.float32)
    summed = lax.psum(jnp.dot(act_low, weight_out, preferred_element_type=jnp.float32), "tp")
    branch = summed + bias_last
    out_rows = ((masked_rows + gamma * branch) * mask_rows).astype(jnp.bfloat16)
    grad_gamma = jnp.sum(grad_rows * branch, axis=0)
    grad_bias_last = jnp.sum(grad_rows * gamma, axis=0)
    branch_low = (grad_rows * gamma).astype(jnp.bfloat16)
    grad_weight_out = contract_rows(act_low, branch_low)
    act_grad = contract_last(branch_low, weight_out)
    pre_grad = act_grad * gelu_slope
    grad_bias_in = jnp.sum(pre_grad, axis=0)
    pre_low = pre_grad.astype(jnp.bfloat16)
    grad_weight_in = contract_rows(adapted, pre_low)
    adapted_grad = lax.psum(contract_last(pre_low, weight_in), "tp")
    grad_scale = contract_rows(hot_rows, adapted_grad * normed, HIGH)
    grad_shift = contract_rows(hot_rows, adapted_grad, HIGH)
    normed_grad = adapted_grad * jnp.dot(hot_rows, scale_table, precision=HIGH)
    mean_grad = jnp.mean(normed_grad, axis=-1, keepdims=True)
    mean_cross = jnp.mean(normed_grad * normed, axis=-1, keepdims=True)
    conv_grad = inv_std * (normed_grad - mean_grad - normed * mean_cross)
    grad_conv_bias = jnp.sum(conv_grad, axis=0)
    tap_grads = []
    for tap_index in range(tap_count):
        shifted = padded[:, tap_index : tap_index + frames].reshape(row_count, model_width)
        tap_grads.append(jnp.sum(conv_grad * shifted, axis=0))
    grad_conv_weight = jnp.stack(tap_grads, axis=0)
    grad_padded = jnp.pad(
        conv_grad.reshape(item_count, frames, model_width),
        ((0, 0), (half_width, half_width), (0, 0)),
    )
    masked_grad = conv_taps[0] * grad_padded[:, 2 * half_width : 2 * half_width + frames]
    for tap_index in range(1, tap_count):
        offset = 2 * half_width - tap_index
        masked_grad = masked_grad + conv_taps[tap_index] * grad_padded[:, offset : offset + frames]
    grad_tokens = frame_mask[..., None] * (
        grad_rows.reshape(item_count, frames, model_width) + masked_grad
    )
    (
        grad_weight_in,
        grad_bias_in,
        grad_weight_out,
        grad_conv_weight,
        grad_conv_bias,
        grad_scale,
        grad_shift,
        grad_bias_last,
        grad_gamma,
    ) = lax.psum(
        (
            grad_weight_in,
            grad_bias_in,
            grad_weight_out,
            grad_conv_weight,
            grad_conv_bias,
            grad_scale,
            grad_shift,
            grad_bias_last,
            grad_gamma,
        ),
        "dp",
    )
    block_out = out_rows.reshape(item_count, frames, model_width)
    return (
        block_out,
        grad_tokens,
        grad_conv_weight,
        grad_conv_bias,
        grad_scale,
        grad_shift,
        grad_weight_in,
        grad_bias_in,
        grad_weight_out,
        grad_bias_last,
        grad_gamma,
    )


def solution(mesh):
    in_specs = (
        P("dp", None, None),
        P("dp"),
        P("dp"),
        P(),
        P(),
        P(),
        P(),
        P(None, "tp"),
        P("tp"),
        P("tp", None),
        P(),
        P(),
        P("dp", None, None),
    )
    out_specs = (
        P("dp", None, None),
        P("dp", None, None),
        P(),
        P(),
        P(),
        P(),
        P(None, "tp"),
        P("tp"),
        P("tp", None),
        P(),
        P(),
    )
    return jax.shard_map(
        per_device, mesh=mesh, in_specs=in_specs, out_specs=out_specs, check_vma=False
    )
```

profile of v0, /device:TPU:0, one launch (start us, length us, event | category | flops | bytes accessed | tf_op | source)
XLA Modules:
  0.0 496.8 jit_solution(17823976869492066244)
XLA Ops:
  7.3 1.0 fusion.34
  8.3 1.0 fusion.24
  9.3 0.7 convert_element_type.68
  10.0 2.6 convert_multiply_fusion
  12.6 21.1 %fusion.33 = (f32[16,256]{1,0:T(8,128)S(1)}, f32[16,256,512]{2,1,0:T(8,128)}, f32[16,256,512]{2,1,0:T(8,128)}, f32[16,256,512]{2,1,0:T(8,128)}, f32[16,256,512]{...) fusion(f32[512]{0:T(512)S(1)} %bitcast.116, f32[512]{0:T(512)S(1)} %bitcast.114, ...), kind=kLoop, calls=%fused_computation.75 | loop fusion | flops 35647488 | bytes 71352320 | tf_op jit(solution)/shard_map/reduce_sum | solution.py:59
  33.9 4.2 multiply_reduce_fusion.3
  39.2 1.3 add_convert_fusion
  40.5 2.9 multiply_convert_fusion.1
  43.5 1.0 copy-done.5
  44.5 1.1 multiply_convert_fusion
  45.6 5.0 %fusion.35 = (f32[384]{0:T(512)}, bf16[4096,384]{1,0:T(8,128)(2,1)S(1)}) fusion(f32[4096,384]{1,0:T(8,128)S(1)} %get-tuple-element.70, bf16[4096,512]{1,0:T(8,128)(2,1)S(1)} %multiply_convert_fusion, bf16[384,512]{1,0:T(8,128)(2,1)S(1)} %copy-done.11), kind=kOutput, calls=%fused_computation.77 | convolution fusion | flops 1627913856 | bytes 14026240 | tf_op jit(solution)/shard_map/dot_general | solution.py:27
  50.7 5.6 %fusion.21 = f32[4096,512]{1,0:T(8,128)} fusion(bf16[512,384]{1,0:T(8,128)(2,1)S(1)} %copy-done, bf16[4096,384]{1,0:T(8,128)(2,1)S(1)} %get-tuple-element.73), kind=kOutput, calls=%fused_computation.56 | convolution fusion | flops 1610612736 | bytes 11927552 | tf_op jit(solution)/shard_map/dot_general | solution.py:27
  56.3 5.7 %fusion.36 = f32[4096,512]{1,0:T(8,128)} fusion(bf16[4096,384]{1,0:T(8,128)(2,1)S(1)} %get-tuple-element.69, bf16[384,512]{1,0:T(8,128)(2,1)S(1)} %copy-done.11), kind=kOutput, calls=%fused_computation.78 | convolution fusion | flops 1610612736 | bytes 11927552 | tf_op jit(solution)/shard_map/dot_general | solution.py:90
  62.3 6.0 %fusion.38 = f32[384,512]{1,0:T(8,128)} fusion(bf16[4096,384]{1,0:T(8,128)(2,1)} %copy-done.10, bf16[4096,512]{1,0:T(8,128)(2,1)} %copy-done.7), kind=kOutput, calls=%fused_computation.80 | convolution fusion | flops 1610612736 | bytes 8126464 | tf_op jit(solution)/shard_map/dot_general | solution.py:17
  68.3 3.2 fusion.19
  71.7 282.0 %all-reduce.10.cloned.1.call-done = (f32[4096,512]{1,0:T(8,128)}, f32[4096,512]{1,0:T(8,128)}) async-done(((f32[4096,512]{1,0:T(8,128)}, f32[4096,512]{1,0:T(8,128)}), (f32[4096,512]{1,0:T(8,128)}, f32[4096,512]{1,0:T(8,128)})) %all-reduce.10.cloned.1.call-update) | async-done | bytes 16777232 | tf_op jit(solution)/shard_map/psum | solution.py:90
  353.8 7.1 %fusion.37 = f32[2,512]{1,0:T(2,128)S(1)} fusion(f32[4096,2]{0,1:T(2,128)S(1)} %bitcast.97, f32[4096,512]{1,0:T(8,128)} %get-tuple-element.31), kind=kOutput, calls=%fused_computation.79 | convolution fusion | flops 50331648 | bytes 8425472 | tf_op jit(solution)/shard_map/dot_general | solution.py:17
  360.9 11.0 %fusion.32 = (f32[4096]{0:T(1024)S(1)}, f32[4096]{0:T(1024)S(1)}, f32[4096,512]{1,0:T(8,128)}) fusion(f32[4096]{0:T(1024)S(1)} %bitcast.102, f32[16,256,512]{2,1,0:T(8,128)} %copy-done.2, f32[4096,512]{1,0:T(8,128)S(1)} %copy-done.4, f32[4096,2]{0,1:T(2,128)S(1)} %bitcast.98, bf16[2,512]{1,0:T(2,128)(2,1)S(1)} %copy-done.32), kind=kOutput, calls=%fused_computation.74 | convolution fusion | flops 60809216 | bytes 25249792 | tf_op jit(solution)/shard_map/dot_general | solution.py:105
  372.0 37.2 %multiply_reduce_fusion = (f32[512]{0:T(512)S(1)}, bf16[4096,512]{1,0:T(8,128)(2,1)}, f32[4096,512]{1,0:T(8,128)}, f32[512]{0:T(512)S(1)}, f32[512]{0:T(512)S(1)...) fusion(bf16[16,256,512]{2,1,0:T(8,128)(2,1)} %param.25, ...), kind=kLoop, calls=%fused_computation.20 | loop fusion | flops 60812800 | bytes 109139968 | tf_op jit(solution)/shard_map/reduce_sum | solution.py:93
  409.2 8.1 %fusion.9 = f32[2,512]{1,0:T(2,128)S(1)} fusion(f32[4096,2]{0,1:T(2,128)S(1)} %bitcast.99, f32[4096,512]{1,0:T(8,128)} %get-tuple-element.31, f32[4096,512]{1,0:T(8,128)} %get-tuple-element.40), kind=kOutput, calls=%fused_computation.22 | convolution fusion | flops 52428800 | bytes 16814080 | tf_op jit(solution)/shard_map/dot_general | solution.py:17
  417.5 30.6 %multiply_reduce_fusion.1 = (f32[512]{0:T(512)S(1)}, f32[16,256,512]{2,1,0:T(8,128)}) fusion(bf16[16,256,512]{2,1,0:T(8,128)(2,1)} %param.25, f32[512]{0:T(512)S(1)} %copy-done.16, f32[16,256]{1,0:T(8,128)S(1)} %get-tuple-element.68, f32[512]{0:T(512)S(1)} %bitcast.117, f32[512]{0:T(512)S(1)} %bitcast.115, f32[512]{0:T(512)S(1)} %bitcast.113, ...), kind=kLoop, calls=%fused_computation.21 | loop fusion | flops 39845376 | bytes 21006336 | tf_op jit(solution)/shard_map/reduce_sum | solution.py:94
  448.1 37.7 %all-reduce.2 = (f32[7,512]{1,0:T(8,128)}, f32[512]{0:T(512)}, f32[2,512]{1,0:T(2,128)}, f32[2,512]{1,0:T(2,128)}, f32[384]{0:T(512)}, /*index=5*/f32[512]{0:T(512)}, f32[512]{0:T(512)}) all-reduce(f32[7,512]{1,0:T(8,128)S(1)} %stack.31, f32[512]{0:T(512)S(1)} %get-tuple-element.48, ...), channel_id=1, replica_groups=mesh['dp'=8,'tp'=4] {'dp'}, use_global_device_ids=true, to_apply=%region_13.14 | all-reduce | flops 7552 | bytes 60416 | tf_op jit(solution)/shard_map/psum | solution.py:136
  485.8 2.1 copy.31
  487.9 2.1 copy.32
  (98 shorter events, 1.7 us)
Async XLA Ops:
  7.2 33.4 %copy-start = (bf16[512,384]{1,0:T(8,128)(2,1)S(1)}, bf16[512,384]{1,0:T(8,128)(2,1)}, u32[]{:S(2)}) copy-start(bf16[512,384]{1,0:T(8,128)(2,1)} %param.20) | copy-start | bytes 1179652
  7.2 346.6 %all-reduce.10.cloned.1.call-start = ((), (), s32[]{:S(2)}) async-start(), calls=%async_computation.1 | async-start | bytes 33554432 | tf_op jit(solution)/shard_map/psum | solution.py:90
  8.2 25.5 %copy-start.17 = (f32[1,512]{1,0:T(1,128)}, f32[1,512]{1,0:T(1,128)S(1)}, u32[]{:S(2)}) copy-start(f32[1,512]{1,0:T(1,128)S(1)} %get-tuple-element.60) | copy-start | bytes 6148
  8.2 25.5 %copy-start.19 = (f32[1,512]{1,0:T(1,128)}, f32[1,512]{1,0:T(1,128)S(1)}, u32[]{:S(2)}) copy-start(f32[1,512]{1,0:T(1,128)S(1)} %get-tuple-element.61) | copy-start | bytes 6148
  8.2 25.5 %copy-start.21 = (f32[1,512]{1,0:T(1,128)}, f32[1,512]{1,0:T(1,128)S(1)}, u32[]{:S(2)}) copy-start(f32[1,512]{1,0:T(1,128)S(1)} %get-tuple-element.62) | copy-start | bytes 6148
  8.3 25.5 %copy-start.23 = (f32[1,512]{1,0:T(1,128)}, f32[1,512]{1,0:T(1,128)S(1)}, u32[]{:S(2)}) copy-start(f32[1,512]{1,0:T(1,128)S(1)} %get-tuple-element.63) | copy-start | bytes 6148
  8.3 25.5 %copy-start.25 = (f32[1,512]{1,0:T(1,128)}, f32[1,512]{1,0:T(1,128)S(1)}, u32[]{:S(2)}) copy-start(f32[1,512]{1,0:T(1,128)S(1)} %get-tuple-element.64) | copy-start | bytes 6148
  8.3 25.5 %copy-start.27 = (f32[1,512]{1,0:T(1,128)}, f32[1,512]{1,0:T(1,128)S(1)}, u32[]{:S(2)}) copy-start(f32[1,512]{1,0:T(1,128)S(1)} %get-tuple-element.65) | copy-start | bytes 6148
  8.3 25.5 %copy-start.29 = (f32[1,512]{1,0:T(1,128)}, f32[1,512]{1,0:T(1,128)S(1)}, u32[]{:S(2)}) copy-start(f32[1,512]{1,0:T(1,128)S(1)} %get-tuple-element.66) | copy-start | bytes 6148
  12.6 21.2 %copy-start.3 = (f32[16,256,512]{2,1,0:T(8,128)}, f32[16,256,512]{2,1,0:T(8,128)S(1)}, u32[]{:S(2)}) copy-start(f32[16,256,512]{2,1,0:T(8,128)S(1)} %convert_multiply_fusion) | copy-start | bytes 25165828
  43.5 12.8 %copy-start.10 = (bf16[4096,384]{1,0:T(8,128)(2,1)}, bf16[4096,384]{1,0:T(8,128)(2,1)S(1)}, u32[]{:S(2)}) copy-start(bf16[4096,384]{1,0:T(8,128)(2,1)S(1)} %get-tuple-element.69) | copy-start | bytes 9437188
  62.1 423.8 %all-reduce.8.cloned.1.call-start = ((), (), s32[]{:S(2)}) async-start(), calls=%async_computation | async-start | bytes 3145728 | tf_op jit(solution)/shard_map/psum | solution.py:136
  68.3 292.6 %copy-start.32 = (bf16[2,512]{1,0:T(2,128)(2,1)S(1)}, bf16[2,512]{1,0:T(2,128)(2,1)}, u32[]{:S(2)}) copy-start(bf16[2,512]{1,0:T(2,128)(2,1)} %param.18) | copy-start | bytes 6148
  360.9 11.1 %copy-start.13 = (f32[2,2,8,128]{3,1,2,0:T(2,128)S(1)}, f32[2,2,8,128]{3,1,2,0:T(2,128)}, u32[]{:S(2)}) copy-start(f32[2,2,8,128]{3,1,2,0:T(2,128)} %copy-done.12) | copy-start | bytes 49156
  360.9 11.0 %copy-start.16 = (f32[512]{0:T(512)S(1)}, f32[512]{0:T(512)}, u32[]{:S(2)}) copy-start(f32[512]{0:T(512)} %copy-done.15) | copy-start | bytes 6148
  409.2 8.3 %copy-start.18 = (f32[1,512]{1,0:T(1,128)S(1)}, f32[1,512]{1,0:T(1,128)}, u32[]{:S(2)}) copy-start(f32[1,512]{1,0:T(1,128)} %copy-done.17) | copy-start | bytes 6148
  409.2 8.3 %copy-start.20 = (f32[1,512]{1,0:T(1,128)S(1)}, f32[1,512]{1,0:T(1,128)}, u32[]{:S(2)}) copy-start(f32[1,512]{1,0:T(1,128)} %copy-done.19) | copy-start | bytes 6148
  409.2 8.3 %copy-start.22 = (f32[1,512]{1,0:T(1,128)S(1)}, f32[1,512]{1,0:T(1,128)}, u32[]{:S(2)}) copy-start(f32[1,512]{1,0:T(1,128)} %copy-done.21) | copy-start | bytes 6148
  409.2 8.3 %copy-start.24 = (f32[1,512]{1,0:T(1,128)S(1)}, f32[1,512]{1,0:T(1,128)}, u32[]{:S(2)}) copy-start(f32[1,512]{1,0:T(1,128)} %copy-done.23) | copy-start | bytes 6148
  409.2 8.3 %copy-start.26 = (f32[1,512]{1,0:T(1,128)S(1)}, f32[1,512]{1,0:T(1,128)}, u32[]{:S(2)}) copy-start(f32[1,512]{1,0:T(1,128)} %copy-done.25) | copy-start | bytes 6148
  409.2 8.3 %copy-start.28 = (f32[1,512]{1,0:T(1,128)S(1)}, f32[1,512]{1,0:T(1,128)}, u32[]{:S(2)}) copy-start(f32[1,512]{1,0:T(1,128)} %copy-done.27) | copy-start | bytes 6148
  409.2 8.3 %copy-start.30 = (f32[1,512]{1,0:T(1,128)S(1)}, f32[1,512]{1,0:T(1,128)}, u32[]{:S(2)}) copy-start(f32[1,512]{1,0:T(1,128)} %copy-done.29) | copy-start | bytes 6148
  417.4 72.5 %copy-start.1 = (bf16[512,384]{1,0:T(8,128)(2,1)S(1)}, bf16[512,384]{1,0:T(8,128)(2,1)}, u32[]{:S(2)}) copy-start(bf16[512,384]{1,0:T(8,128)(2,1)} %param.20) | copy-start | bytes 1179652
  417.5 30.6 %copy-start.36 = (f32[384]{0:T(512)S(1)}, f32[384]{0:T(512)}, u32[]{:S(2)}) copy-start(f32[384]{0:T(512)} %get-tuple-element.72) | copy-start | bytes 4612
  (18 other events, 82.5 us)
Sparse Core Ops, SparseCore 0:
  62.2 291.5 all-reduce.9
  358.5 89.2 all-reduce.7
where the time goes:
time: 497 us
  waiting for transfers between devices  282 us (57%)
  other arithmetic  100 us (20%)
  matrix products  55.2 us (11%)
  blocking collectives  37.7 us (8%)
  between operations  14.7 us (3%)
  local copies, waits for them, and re-layouts  6.43 us (1%)
    psum x1, waiting for transfers between devices, per_device(): lax.psum(jnp.dot(act_low, weight_out, preferred_element_type=jnp.float32)...  282 us
    psum x1, blocking collectives, per_device(): lax.psum((grad_weight_in, grad_bias_in, grad_weight_out, grad_conv_weight...  37.7 us
    reduce_sum x1, other arithmetic, per_device(): grad_gamma = jnp.sum(grad_rows * branch, axis=0)  37.2 us
    reduce_sum x1, other arithmetic, per_device(): grad_bias_last = jnp.sum(grad_rows * gamma, axis=0)  30.6 us
    dot_general x4, matrix products, contract_rows(): lax.dot_general(left, right, (((0,), (0,)), ((), ())), precision=precisio...  24.5 us
    reduce_sum x1, other arithmetic, per_device(): row_mean = jnp.mean(conv, axis=-1, keepdims=True)  21.1 us
    dot_general x1, matrix products, per_device(): normed_grad = adapted_grad * jnp.dot(hot_rows, scale_table, precision=HIGH)  11 us
    dot_general x2, matrix products, contract_last(): lax.dot_general(left, right, (((1,), (1,)), ((), ())), preferred_element_...  10.6 us
  transfers between devices with their start and end apart: 2, of which 1 were waited for; matrix products, arithmetic and copies ran while one was open for 21% of the time, Pallas kernels for 0%

commit v1 on v0

--- a/solution.py
+++ b/solution.py
@@ -87,7 +87,10 @@
     grad_rows = cotangent.astype(jnp.float32).reshape(row_count, model_width) * mask_rows
     gamma = layer_scale.astype(jnp.float32)
     bias_last = bias_out.astype(jnp.float32)
-    summed = lax.psum(jnp.dot(act_low, weight_out, preferred_element_type=jnp.float32), "tp")
+    summed = jnp.sum(
+        lax.all_gather(jnp.dot(act_low, weight_out, preferred_element_type=jnp.float32), "tp"),
+        axis=0,
+    )
     branch = summed + bias_last
     out_rows = ((masked_rows + gamma * branch) * mask_rows).astype(jnp.bfloat16)
     grad_gamma = jnp.sum(grad_rows * branch, axis=0)

time: 497 us -> 523 us (1.052)
  other arithmetic: 100 us -> 125 us
    psum x1, waiting for transfers between devices: 282 us -> 140 us  [per_device(): adapted_grad = lax.psum(contract_last(pre_low, weight_in), 'tp')]
    all_gather x0 -> x1, waiting for transfers between devices: none -> 139 us  [per_device(): lax.all_gather(jnp.dot(act_low, weight_out, preferred_element_type=jnp.fl...]
    reduce_sum x1 -> x2, other arithmetic: 30.6 us -> 55.3 us  [the longest x1 38.5 us: per_device(): grad_conv_bias = jnp.sum(conv_grad, axis=0)]
  transfers between devices with their start and end apart: 2 -> 3, of which waited for: 1 -> 3; matrix products, arithmetic and copies ran while one was open for 21% -> 26% of each run, Pallas kernels for 0% -> 0%
where the time goes in v1:
time: 523 us; the launch traced here: 522 us
  waiting for transfers between devices  281 us (54%)
  other arithmetic  125 us (24%)
  matrix products  55.1 us (11%)
  blocking collectives  38.2 us (7%)
  between operations  14.3 us (3%)
  local copies, waits for them, and re-layouts  8.75 us (2%)
    psum x1, waiting for transfers between devices, per_device(): adapted_grad = lax.psum(contract_last(pre_low, weight_in), 'tp')  140 us
    all_gather x1, waiting for transfers between devices, per_device(): lax.all_gather(jnp.dot(act_low, weight_out, preferred_element_type=jnp.fl...  139 us
    reduce_sum x1, other arithmetic, per_device(): grad_conv_bias = jnp.sum(conv_grad, axis=0)  38.5 us
    psum x1, blocking collectives, per_device(): lax.psum((grad_weight_in, grad_bias_in, grad_weight_out, grad_conv_weight...  38.2 us
    reduce_sum x1, other arithmetic, per_device(): grad_gamma = jnp.sum(grad_rows * branch, axis=0)  36.7 us
    dot_general x4, matrix products, contract_rows(): lax.dot_general(left, right, (((0,), (0,)), ((), ())), precision=precisio...  22.5 us
    reduce_sum x1, other arithmetic, per_device(): row_mean = jnp.mean(conv, axis=-1, keepdims=True)  21.1 us
    reduce_sum x1, other arithmetic, per_device(): jnp.sum(lax.all_gather(jnp.dot(act_low, weight_out, preferred_element_typ...  16.8 us
  transfers between devices with their start and end apart: 3, of which 3 were waited for; matrix products, arithmetic and copies ran while one was open for 26% of the time, Pallas kernels for 0%

profile of v1, /device:TPU:0, one launch (start us, length us, event | category | flops | bytes accessed | tf_op | source)
XLA Modules:
  0.0 522.2 jit_solution(17740309782703085176)
XLA Ops:
  10.0 2.6 convert_multiply_fusion
  12.6 21.1 %fusion.33 = (f32[16,256]{1,0:T(8,128)S(1)}, f32[16,256,512]{2,1,0:T(8,128)}, f32[16,256,512]{2,1,0:T(8,128)}, f32[16,256,512]{2,1,0:T(8,128)}, f32[16,256,512]{...) fusion(f32[512]{0:T(512)S(1)} %bitcast.113, f32[512]{0:T(512)S(1)} %bitcast.111, ...), kind=kLoop, calls=%fused_computation.73 | loop fusion | flops 35647488 | bytes 71352320 | tf_op jit(solution)/shard_map/reduce_sum | solution.py:59
  33.9 4.2 multiply_reduce_fusion.3
  39.2 1.3 add_convert_fusion
  40.5 2.9 multiply_convert_fusion.1
  44.5 1.1 fusion.8
  45.6 5.1 fusion.35
  50.6 1.6 copy-done.10
  52.3 5.6 %fusion.21 = f32[4096,512]{1,0:T(8,128)} fusion(bf16[512,384]{1,0:T(8,128)(2,1)S(1)} %copy-done, bf16[4096,384]{1,0:T(8,128)(2,1)S(1)} %get-tuple-element.61), kind=kOutput, calls=%fused_computation.54 | convolution fusion | flops 1610612736 | bytes 11927552 | tf_op jit(solution)/shard_map/dot_general | solution.py:27
  58.8 5.7 %fusion.36 = f32[4096,512]{1,0:T(8,128)} fusion(bf16[4096,384]{1,0:T(8,128)(2,1)S(1)} %get-tuple-element.57, bf16[384,512]{1,0:T(8,128)(2,1)S(1)} %copy-done.13), kind=kOutput, calls=%fused_computation.76 | convolution fusion | flops 1610612736 | bytes 11927552 | tf_op jit(solution)/shard_map/dot_general | solution.py:91
  64.7 5.8 %fusion.38 = f32[384,512]{1,0:T(8,128)} fusion(bf16[4096,384]{1,0:T(8,128)(2,1)S(1)} %get-tuple-element.57, bf16[4096,512]{1,0:T(8,128)(2,1)} %copy-done.7), kind=kOutput, calls=%fused_computation.78 | convolution fusion | flops 1610612736 | bytes 8126464 | tf_op jit(solution)/shard_map/dot_general | solution.py:17
  70.5 3.2 fusion.19
  73.9 139.6 %all-reduce.7.cloned.1.call-done = f32[4096,512]{1,0:T(8,128)} async-done(((f32[4096,512]{1,0:T(8,128)}), f32[4096,512]{1,0:T(8,128)}) %all-reduce.7.cloned.1.call-update) | async-done | bytes 8388624 | tf_op jit(solution)/shard_map/psum | solution.py:105
  213.6 12.9 %fusion.32 = (f32[4096]{0:T(1024)S(1)}, f32[4096]{0:T(1024)S(1)}, f32[4096,512]{1,0:T(8,128)}) fusion(f32[4096]{0:T(1024)S(1)} %bitcast.98, f32[16,256,512]{2,1,0:T(8,128)} %copy-done.2, f32[4096,512]{1,0:T(8,128)} %all-reduce.7.cloned.1.call-done, f32[4096,2]{0,1:T(2,128)S(1)} %bitcast.95, bf16[2,512]{1,0:T(2,128)(2,1)S(1)} %copy-done.32), kind=kOutput, calls=%fused_computation.72 | convolution fusion | flops 60809216 | bytes 25249792 | tf_op jit(solution)/shard_map/dot_general | solution.py:108
  226.5 38.5 %fusion.31 = (f32[512]{0:T(512)S(1)}, f32[512]{0:T(512)S(1)}, f32[512]{0:T(512)S(1)}, f32[512]{0:T(512)S(1)}, f32[512]{0:T(512)S(1)}, /*index=5*/f32[512]{0:T(51...) fusion(f32[16,256,512]{2,1,0:T(8,128)} %get-tuple-element.43, ...), kind=kLoop, calls=%fused_computation.71 | loop fusion | flops 41938944 | bytes 92340224 | tf_op jit(solution)/shard_map/reduce_sum | solution.py:112
  265.0 6.5 %fusion.37 = f32[2,512]{1,0:T(2,128)S(1)} fusion(f32[4096,2]{0,1:T(2,128)S(1)} %bitcast.96, f32[4096,512]{1,0:T(8,128)} %all-reduce.7.cloned.1.call-done), kind=kOutput, calls=%fused_computation.77 | convolution fusion | flops 50331648 | bytes 8425472 | tf_op jit(solution)/shard_map/dot_general | solution.py:17
  271.6 6.9 %fusion.9 = f32[2,512]{1,0:T(2,128)S(1)} fusion(f32[4096,2]{0,1:T(2,128)S(1)} %bitcast.97, f32[4096,512]{1,0:T(8,128)} %all-reduce.7.cloned.1.call-done, f32[4096,512]{1,0:T(8,128)S(1)} %copy-done.5), kind=kOutput, calls=%fused_computation.21 | convolution fusion | flops 52428800 | bytes 16814080 | tf_op jit(solution)/shard_map/dot_general | solution.py:17
  278.5 138.9 %all-gather.3.cloned.1.call-done = f32[16384,512]{1,0:T(8,128)} async-done(((f32[4096,512]{1,0:T(8,128)}), f32[16384,512]{1,0:T(8,128)}) %all-gather.3.cloned.1.call-update) | async-done | bytes 33554448 | tf_op jit(solution)/shard_map/all_gather | solution.py:91
  417.5 16.8 %reduce_sum.148 = f32[4096,512]{1,0:T(8,128)} reduce(f32[4,4096,512]{2,1,0:T(8,128)} %bitcast.91, f32[]{:T(128)} %constant.8.clone.1), dimensions={0}, to_apply=%region_2.3 | reduce | flops 6291456 | bytes 41943044 | tf_op jit(solution)/shard_map/reduce_sum | solution.py:90
  434.4 36.7 %multiply_reduce_fusion = (f32[512]{0:T(512)S(1)}, f32[512]{0:T(512)S(1)}, f32[16,256,512]{2,1,0:T(8,128)}, bf16[16,256,512]{2,1,0:T(8,128)(2,1)}) fusion(f32[4096,512]{1,0:T(8,128)} %reduce_sum.148, bf16[16,256,512]{2,1,0:T(8,128)(2,1)} %param.25, f32[512]{0:T(512)S(1)} %convert_element_type.74, f32[16,256]{1,0:T(8,128)S(1)} %get-tuple-element.56, ...), kind=kLoop, calls=%fused_computation.19 | loop fusion | flops 58719232 | bytes 37787648 | tf_op jit(solution)/shard_map/reduce_sum | solution.py:96
  471.1 38.2 %all-reduce.2 = (f32[7,512]{1,0:T(8,128)}, f32[512]{0:T(512)}, f32[2,512]{1,0:T(2,128)}, f32[2,512]{1,0:T(2,128)}, f32[384]{0:T(512)}, /*index=5*/f32[512]{0:T(512)}, f32[512]{0:T(512)}) all-reduce(f32[7,512]{1,0:T(8,128)S(1)} %stack.31, f32[512]{0:T(512)S(1)} %get-tuple-element.11, ...), channel_id=1, replica_groups=mesh['dp'=8,'tp'=4] {'dp'}, use_global_device_ids=true, to_apply=%region_13.14 | all-reduce | flops 7552 | bytes 60416 | tf_op jit(solution)/shard_map/psum | solution.py:139
  509.3 2.2 all-reduce.9.cloned.1.call-done
  511.5 2.1 copy.30
  513.6 2.1 copy.31
  (102 shorter events, 6.2 us)
Async XLA Ops:
  7.2 33.3 %copy-start = (bf16[512,384]{1,0:T(8,128)(2,1)S(1)}, bf16[512,384]{1,0:T(8,128)(2,1)}, u32[]{:S(2)}) copy-start(bf16[512,384]{1,0:T(8,128)(2,1)} %param.20) | copy-start | bytes 1179652
  7.2 206.4 %all-reduce.7.cloned.1.call-start = ((), (), s32[]{:S(2)}) async-start(), calls=%async_computation | async-start | bytes 16777216 | tf_op jit(solution)/shard_map/psum | solution.py:105
  8.2 25.5 %copy-start.15 = (f32[1,512]{1,0:T(1,128)}, f32[1,512]{1,0:T(1,128)S(1)}, u32[]{:S(2)}) copy-start(f32[1,512]{1,0:T(1,128)S(1)} %get-tuple-element.48) | copy-start | bytes 6148
  8.2 25.5 %copy-start.17 = (f32[1,512]{1,0:T(1,128)}, f32[1,512]{1,0:T(1,128)S(1)}, u32[]{:S(2)}) copy-start(f32[1,512]{1,0:T(1,128)S(1)} %get-tuple-element.49) | copy-start | bytes 6148
  8.2 25.5 %copy-start.19 = (f32[1,512]{1,0:T(1,128)}, f32[1,512]{1,0:T(1,128)S(1)}, u32[]{:S(2)}) copy-start(f32[1,512]{1,0:T(1,128)S(1)} %get-tuple-element.50) | copy-start | bytes 6148
  8.3 25.5 %copy-start.21 = (f32[1,512]{1,0:T(1,128)}, f32[1,512]{1,0:T(1,128)S(1)}, u32[]{:S(2)}) copy-start(f32[1,512]{1,0:T(1,128)S(1)} %get-tuple-element.51) | copy-start | bytes 6148
  8.3 25.5 %copy-start.23 = (f32[1,512]{1,0:T(1,128)}, f32[1,512]{1,0:T(1,128)S(1)}, u32[]{:S(2)}) copy-start(f32[1,512]{1,0:T(1,128)S(1)} %get-tuple-element.52) | copy-start | bytes 6148
  8.3 25.5 %copy-start.25 = (f32[1,512]{1,0:T(1,128)}, f32[1,512]{1,0:T(1,128)S(1)}, u32[]{:S(2)}) copy-start(f32[1,512]{1,0:T(1,128)S(1)} %get-tuple-element.53) | copy-start | bytes 6148
  8.3 25.5 %copy-start.27 = (f32[1,512]{1,0:T(1,128)}, f32[1,512]{1,0:T(1,128)S(1)}, u32[]{:S(2)}) copy-start(f32[1,512]{1,0:T(1,128)S(1)} %get-tuple-element.54) | copy-start | bytes 6148
  12.6 21.1 %copy-start.3 = (f32[16,256,512]{2,1,0:T(8,128)}, f32[16,256,512]{2,1,0:T(8,128)S(1)}, u32[]{:S(2)}) copy-start(f32[16,256,512]{2,1,0:T(8,128)S(1)} %convert_multiply_fusion) | copy-start | bytes 25165828
  57.9 359.6 %all-gather.3.cloned.1.call-start = ((), (), s32[]{:S(2)}) async-start(), calls=%async_computation.1 | async-start | bytes 41943040 | tf_op jit(solution)/shard_map/all_gather | solution.py:91
  64.6 446.9 %all-reduce.9.cloned.1.call-start = ((), (), s32[]{:S(2)}) async-start(), calls=%async_computation.2 | async-start | bytes 3145728 | tf_op jit(solution)/shard_map/psum | solution.py:139
  70.5 143.1 %copy-start.32 = (bf16[2,512]{1,0:T(2,128)(2,1)S(1)}, bf16[2,512]{1,0:T(2,128)(2,1)}, u32[]{:S(2)}) copy-start(bf16[2,512]{1,0:T(2,128)(2,1)} %param.18) | copy-start | bytes 6148
  265.0 6.5 %copy-start.5 = (f32[4096,512]{1,0:T(8,128)S(1)}, f32[4096,512]{1,0:T(8,128)}, u32[]{:S(2)}) copy-start(f32[4096,512]{1,0:T(8,128)} %get-tuple-element.37) | copy-start | bytes 25165828
  417.4 16.9 %copy-start.16 = (f32[1,512]{1,0:T(1,128)S(1)}, f32[1,512]{1,0:T(1,128)}, u32[]{:S(2)}) copy-start(f32[1,512]{1,0:T(1,128)} %copy-done.15) | copy-start | bytes 6148
  417.4 16.9 %copy-start.18 = (f32[1,512]{1,0:T(1,128)S(1)}, f32[1,512]{1,0:T(1,128)}, u32[]{:S(2)}) copy-start(f32[1,512]{1,0:T(1,128)} %copy-done.17) | copy-start | bytes 6148
  417.4 16.9 %copy-start.20 = (f32[1,512]{1,0:T(1,128)S(1)}, f32[1,512]{1,0:T(1,128)}, u32[]{:S(2)}) copy-start(f32[1,512]{1,0:T(1,128)} %copy-done.19) | copy-start | bytes 6148
  417.4 16.9 %copy-start.22 = (f32[1,512]{1,0:T(1,128)S(1)}, f32[1,512]{1,0:T(1,128)}, u32[]{:S(2)}) copy-start(f32[1,512]{1,0:T(1,128)} %copy-done.21) | copy-start | bytes 6148
  417.4 16.9 %copy-start.24 = (f32[1,512]{1,0:T(1,128)S(1)}, f32[1,512]{1,0:T(1,128)}, u32[]{:S(2)}) copy-start(f32[1,512]{1,0:T(1,128)} %copy-done.23) | copy-start | bytes 6148
  417.4 16.9 %copy-start.26 = (f32[1,512]{1,0:T(1,128)S(1)}, f32[1,512]{1,0:T(1,128)}, u32[]{:S(2)}) copy-start(f32[1,512]{1,0:T(1,128)} %copy-done.25) | copy-start | bytes 6148
  417.4 16.9 %copy-start.28 = (f32[1,512]{1,0:T(1,128)S(1)}, f32[1,512]{1,0:T(1,128)}, u32[]{:S(2)}) copy-start(f32[1,512]{1,0:T(1,128)} %copy-done.27) | copy-start | bytes 6148
  417.5 16.9 %copy-start.30 = (f32[512]{0:T(512)S(1)}, f32[512]{0:T(512)}, u32[]{:S(2)}) copy-start(f32[512]{0:T(512)} %copy-done.29) | copy-start | bytes 6148
  434.4 36.7 %copy-start.36 = (f32[384]{0:T(512)S(1)}, f32[384]{0:T(512)}, u32[]{:S(2)}) copy-start(f32[384]{0:T(512)} %get-tuple-element.60) | copy-start | bytes 4612
  434.4 81.3 %copy-start.1 = (bf16[512,384]{1,0:T(8,128)(2,1)S(1)}, bf16[512,384]{1,0:T(8,128)(2,1)}, u32[]{:S(2)}) copy-start(bf16[512,384]{1,0:T(8,128)(2,1)} %param.20) | copy-start | bytes 1179652
  (19 other events, 79.2 us)
Sparse Core Ops, SparseCore 0:
  58.0 155.5 all-reduce.6
  215.7 201.6 all-gather.2
  422.1 89.3 all-reduce.8
